TPU v7x, 32 devices: a whole 2x2x4 slice. The times are simulated.
32 devices in a mesh: gx: 2 (over x), gy: 4 (over z), gz: 4 (over y, core).
Axes of the slice: x: 2, y: 2, z: 4, core: 2. Of those that a mesh axis runs over, the one named last changes fastest.
Arguments:
- volume: float32 [16, 8, 64, 512], P(None, 'gx', 'gy', 'gz'), may hold values from -26 to 26
- weight: float32 [16, 16, 3, 3, 3], replicated, may hold values from -0.3125 to 0.3125
- gamma: float32 [16], replicated, may hold values from 0.5 to 1.5
- beta: float32 [16], replicated, may hold values from -0.5 to 0.5
- cotangent: float32 [16, 8, 64, 512], P(None, 'gx', 'gy', 'gz'), may hold values from -6 to 6
Outputs:
- input_grad: float32 [16, 8, 64, 512], P(None, 'gx', 'gy', 'gz')
- weight_grad: float32 [16, 16, 3, 3, 3], replicated
- gamma_grad: float32 [16], replicated
- beta_grad: float32 [16], replicated
All inputs are finite; a program needn't handle non-finite values.
Results may differ from a plain program's by a relative error of at most 0.0003.
Values sent between devices are 32-bit elements; how exact they have to be, the bound alone decides.
No kernel may reach another device: no remote copies, remote signals or barrier semaphores. Data moves between devices by JAX's collectives and lax.ppermute only.
A program may use at most 64 MiB of HBM per device.

v0:
```python
import jax
import jax.numpy as jnp
from jax import lax
from jax.sharding import PartitionSpec as P


def with_halo(block, sides, width):
    for axis, dim in sides:
        count = lax.axis_size(axis)
        forward = [(i, i + 1) for i in range(count - 1)]
        forward.append((count - 1, 0))
        backward = [(target, source) for source, target in forward]
        low = lax.ppermute(
            lax.slice_in_dim(block, block.shape[dim] - width, None, axis=dim), axis, forward
        )
        high = lax.ppermute(lax.slice_in_dim(block, 0, width, axis=dim), axis, backward)
        block = jnp.concatenate([low, block, high], axis=dim)
    return block


def mix(kernel, slab):
    return jnp.einsum("oi,ixyz->oxyz", kernel, slab, precision=lax.Precision.HIGHEST)


def contract(left, slab):
    return jnp.einsum("oxyz,ixyz->oi", left, slab, precision=lax.Precision.HIGHEST)


def shards(volume, weight, gamma, beta, cotangent):
    chans, cells_x, cells_y, cells_z = volume.shape
    count = float(
        cells_x
        * cells_y
        * cells_z
        * lax.axis_size("gx")
        * lax.axis_size("gy")
        * lax.axis_size("gz")
    )
    padded = with_halo(volume, (("gx", 1), ("gy", 2), ("gz", 3)), 1)

    def window(source, first, second, third):
        return source[
            :, first : first + cells_x, second : second + cells_y, third : third + cells_z
        ]

    conv = jnp.zeros(volume.shape, jnp.float32)
    for first in range(3):
        for second in range(3):
            for third in range(3):
                conv = conv + mix(
                    weight[:, :, first, second, third], window(padded, first, second, third)
                )
    first_sum, square_sum = lax.psum(
        (jnp.sum(conv, axis=(1, 2, 3)), jnp.sum(conv * conv, axis=(1, 2, 3))), ("gx", "gy", "gz")
    )
    mean = first_sum / count
    var = square_sum / count - mean * mean
    centred = conv - mean[:, None, None, None]
    rstd = lax.rsqrt(var + 1e-05)
    normed = centred * rstd[:, None, None, None]
    act = gamma[:, None, None, None] * normed + beta[:, None, None, None]
    sig = jax.nn.sigmoid(act)
    act_grad = cotangent * sig * (1.0 + act * (1.0 - sig))
    scale = gamma * rstd
    gamma_grad, beta_grad = lax.psum(
        (jnp.sum(act_grad * normed, axis=(1, 2, 3)), jnp.sum(act_grad, axis=(1, 2, 3))),
        ("gx", "gy", "gz"),
    )
    conv_grad = scale[:, None, None, None] * (
        act_grad
        - (beta_grad / count)[:, None, None, None]
        - normed * (gamma_grad / count)[:, None, None, None]
    )
    pieces = []
    for first in range(3):
        for second in range(3):
            for third in range(3):
                pieces.append(contract(conv_grad, window(padded, first, second, third)))
    weight_grad = lax.psum(
        jnp.stack(pieces, axis=2).reshape(chans, chans, 3, 3, 3), ("gx", "gy", "gz")
    )
    grad_padded = with_halo(conv_grad, (("gx", 1), ("gy", 2), ("gz", 3)), 1)
    input_grad = jnp.zeros(volume.shape, jnp.float32)
    for first in range(3):
        for second in range(3):
            for third in range(3):
                input_grad = input_grad + mix(
                    weight[:, :, first, second, third].T,
                    window(grad_padded, 2 - first, 2 - second, 2 - third),
                )
    return (input_grad, weight_grad, gamma_grad, beta_grad)


def solution(mesh):
    return jax.shard_map(
        shards,
        mesh=mesh,
        in_specs=(P(None, "gx", "gy", "gz"), P(), P(), P(), P(None, "gx", "gy", "gz")),
        out_specs=(P(None, "gx", "gy", "gz"), P(), P(), P()),
        check_vma=False,
    )
```

profile of v0, /device:TPU:0, one launch (start us, length us, event | category | flops | bytes accessed | tf_op | source)
XLA Modules:
  0.0 250.0 jit_solution(15097560473422288166)
XLA Ops:
  0.6 1.1 fusion.319
  1.7 3.0 %collective-permute-start = (f32[16,1,16,128]{3,0,2,1:T(8,128)S(1)}, f32[16,1,16,128]{3,0,2,1:T(8,128)S(1)}, u32[]{:S(2)}, u32[]{:S(2)}) collective-permute-start(f32[16,1,16,128]{3,0,2,1:T(8,128)S(1)} %copy.207), channel_id=1, source_target_pairs={{0,16},{16,0},{1,17},{17,1},{2,18},{18,2},{3,19},{19,3},{4,20},{20... | collective-permute-start | bytes 393224 | tf_op jit(solution)/shard_map/ppermute | solution.py:13
  4.9 2.7 %fusion.206 = f32[16,4,16,128]{3,0,2,1:T(8,128)} fusion(f32[16,16,3,3,3]{1,0,4,3,2:T(8,128)} %param.6, f32[16,4,16,128]{3,2,1,0:T(8,128)} %param.5), kind=kOutput, calls=%fused_computation.290 | convolution fusion | flops 25165824 | bytes 1056768 | tf_op jit(solution)/shard_map/oi,ixyz->oxyz/dot_general | solution.py:22
  7.6 1.5 collective-permute-done
  9.5 1.6 collective-permute-done.1
  11.1 1.9 collective-permute-start.2
  13.0 2.1 collective-permute-start.3
  15.1 2.1 fusion.225
  17.2 2.1 convolution_bitcast_fusion.4
  21.0 1.9 collective-permute-start.5
  22.9 2.1 fusion.85
  25.0 2.1 fusion.86
  27.1 2.1 fusion.87
  29.1 2.1 convolution_bitcast_fusion.3
  31.2 2.1 convolution_bitcast_fusion.5
  33.3 2.1 convolution_bitcast_fusion.6
  36.1 1.6 copy.51
  37.7 1.8 maximum_maximum_fusion
  47.1 1.1 convolution_bitcast_fusion.18
  50.1 1.0 fusion.44
  51.6 1.2 fusion.312
  52.8 38.9 %all-reduce.1 = (f32[16]{0:T(128)S(1)}, f32[16]{0:T(128)S(1)}) all-reduce(f32[16]{0:T(128)S(1)} %get-tuple-element.15, f32[16]{0:T(128)S(1)} %get-tuple-element.14), channel_id=1, replica_groups=mesh['gx'=2,'gy'=4,'gz'=4] {'gx','gy','gz'}, use_global_device_ids=true, to_apply=%region_1.0 | all-reduce | flops 32 | bytes 256 | tf_op jit(solution)/shard_map/psum | solution.py:53
  91.7 2.4 fusion.311
  94.1 40.5 %all-reduce = (f32[16]{0:T(128)S(1)}, f32[16]{0:T(128)S(1)}) all-reduce(f32[16]{0:T(128)S(1)} %get-tuple-element.13, f32[16]{0:T(128)S(1)} %get-tuple-element.12), channel_id=1, replica_groups=mesh['gx'=2,'gy'=4,'gz'=4] {'gx','gy','gz'}, use_global_device_ids=true, to_apply=%region_7.0 | all-reduce | flops 32 | bytes 256 | tf_op jit(solution)/shard_map/psum | solution.py:65
  134.6 1.4 subtract_multiply_fusion
  147.4 1.0 fusion.64
  160.2 41.9 %psum.39 = f32[16,16,3,3,3]{1,0,4,3,2:T(8,128)} all-reduce(f32[16,16,3,3,3]{1,0,4,3,2:T(8,128)} %bitcast.644), channel_id=1, replica_groups=mesh['gx'=2,'gy'=4,'gz'=4] {'gx','gy','gz'}, use_global_device_ids=true, to_apply=%region_8.0 | all-reduce | flops 6912 | bytes 55296 | tf_op jit(solution)/shard_map/psum | solution.py:79
  202.1 1.6 collective-permute-start.6
  204.2 1.4 fusion.204
  205.6 2.5 collective-permute-done.6
  208.0 1.4 collective-permute-done.7
  209.4 2.2 collective-permute-start.9
  211.7 1.4 fusion.78
  213.7 3.9 %collective-permute-done.8 = f32[16,6,1,128]{3,0,2,1:T(8,128)S(1)} collective-permute-done((f32[16,6,1,128]{3,0,2,1:T(8,128)S(1)}, f32[16,6,1,128]{3,0,2,1:T(8,128)S(1)}, u32[]{:S(2)}, u32[]{:S(2)}) %collective-permute-start.8) | collective-permute-done | bytes 49184 | tf_op jit(solution)/shard_map/ppermute | solution.py:13
  217.6 1.2 fusion.315
  218.8 1.8 copy.56
  221.9 1.4 fusion.177
  223.3 1.4 fusion.175
  224.7 1.4 fusion.176
  226.1 1.4 fusion.174
  227.5 1.4 convolution_bitcast_fusion.2
  228.9 1.4 convolution_bitcast_fusion
  230.3 1.6 copy.57
  231.9 1.6 copy.61
  233.5 2.0 pad_maximum_fusion.3
  246.5 1.1 fusion.46
  247.8 1.0 fusion.48
  248.8 1.0 copy.88
  (158 shorter events, 49.1 us)
Async XLA Ops:
  0.6 8.5 %copy-start.2 = (f32[16,4,16,128]{3,2,1,0:T(8,128)S(1)}, f32[16,4,16,128]{3,2,1,0:T(8,128)}, u32[]{:S(2)}) copy-start(f32[16,4,16,128]{3,2,1,0:T(8,128)} %param.5) | copy-start | bytes 1572868
  1.7 7.4 %collective-permute-start = (f32[16,1,16,128]{3,0,2,1:T(8,128)S(1)}, f32[16,1,16,128]{3,0,2,1:T(8,128)S(1)}, u32[]{:S(2)}, u32[]{:S(2)}) collective-permute-start(f32[16,1,16,128]{3,0,2,1:T(8,128)S(1)} %copy.207), channel_id=1, source_target_pairs={{0,16},{16,0},{1,17},{17,1},{2,18},{18,2},{3,19},{19,3},{4,20},{20... | collective-permute-start | bytes 393224 | tf_op jit(solution)/shard_map/ppermute | solution.py:13
  4.8 6.3 %collective-permute-start.1 = (f32[16,1,16,128]{3,0,2,1:T(8,128)S(1)}, f32[16,1,16,128]{3,0,2,1:T(8,128)S(1)}, u32[]{:S(2)}, u32[]{:S(2)}) collective-permute-start(f32[16,1,16,128]{3,0,2,1:T(8,128)S(1)} %copy.208), channel_id=1, source_target_pairs={{16,0},{0,16},{17,1},{1,17},{18,2},{2,18},{19,3},{3,19},{20,4},{4,... | collective-permute-start | bytes 393224 | tf_op jit(solution)/shard_map/ppermute | solution.py:16
  9.5 9.7 %copy-start.7 = (f32[16,5,16,128]{3,0,2,1:T(8,128)}, f32[16,5,16,128]{3,0,2,1:T(8,128)S(1)}, u32[]{:S(2)}) copy-start(f32[16,5,16,128]{3,0,2,1:T(8,128)S(1)} %get-tuple-element.37) | copy-start | bytes 1966084
  11.1 8.1 %copy-start.5 = (f32[16,5,16,128]{3,0,2,1:T(8,128)}, f32[16,5,16,128]{3,0,2,1:T(8,128)S(1)}, u32[]{:S(2)}) copy-start(f32[16,5,16,128]{3,0,2,1:T(8,128)S(1)} %get-tuple-element.44) | copy-start | bytes 1966084
  11.1 8.1 %collective-permute-start.2 = (f32[16,6,1,128]{3,0,2,1:T(8,128)S(1)}, f32[16,6,1,128]{3,0,2,1:T(8,128)S(1)}, u32[]{:S(2)}, u32[]{:S(2)}) collective-permute-start(f32[16,6,1,128]{3,0,2,1:T(8,128)S(1)} %get-tuple-element.33), channel_id=1, source_target_pairs={{0,4},{4,8},{8,12},{12,0},{1,5},{5,9},{9,13},{13,1},{2,6},{6,10},{... | collective-permute-start | bytes 147464 | tf_op jit(solution)/shard_map/ppermute | solution.py:13
  13.0 6.2 %collective-permute-start.3 = (f32[16,6,1,128]{3,0,2,1:T(8,128)S(1)}, f32[16,6,1,128]{3,0,2,1:T(8,128)S(1)}, u32[]{:S(2)}, u32[]{:S(2)}) collective-permute-start(f32[16,6,1,128]{3,0,2,1:T(8,128)S(1)} %get-tuple-element.34), channel_id=1, source_target_pairs={{4,0},{8,4},{12,8},{0,12},{5,1},{9,5},{13,9},{1,13},{6,2},{10,6},{... | collective-permute-start | bytes 147464 | tf_op jit(solution)/shard_map/ppermute | solution.py:16
  20.3 15.1 %collective-permute-start.4 = (f32[16,6,18,1]{2,0,3,1:T(8,128)S(1)}, f32[16,6,18,1]{2,0,3,1:T(8,128)S(1)}, u32[]{:S(2)}, u32[]{:S(2)}) collective-permute-start(f32[16,6,18,1]{2,0,3,1:T(8,128)S(1)} %copy.48), channel_id=1, source_target_pairs={{0,1},{1,2},{2,3},{3,0},{4,5},{5,6},{6,7},{7,4},{8,9},{9,10},{10,1... | collective-permute-start | bytes 20744 | tf_op jit(solution)/shard_map/ppermute | solution.py:13
  21.0 15.1 %collective-permute-start.5 = (f32[16,6,18,1]{2,0,3,1:T(8,128)S(1)}, f32[16,6,18,1]{2,0,3,1:T(8,128)S(1)}, u32[]{:S(2)}, u32[]{:S(2)}) collective-permute-start(f32[16,6,18,1]{2,0,3,1:T(8,128)S(1)} %copy.50), channel_id=1, source_target_pairs={{1,0},{2,1},{3,2},{0,3},{5,4},{6,5},{7,6},{4,7},{9,8},{10,9},{11,1... | collective-permute-start | bytes 20744 | tf_op jit(solution)/shard_map/ppermute | solution.py:16
  37.7 1.8 copy-start.26
  39.5 11.6 %copy-start = (f32[16,6,18,129]{3,0,2,1:T(8,128)}, f32[16,6,18,129]{3,0,2,1:T(8,128)S(1)}, u32[]{:S(2)}) copy-start(f32[16,6,18,129]{3,0,2,1:T(8,128)S(1)} %get-tuple-element.28) | copy-start | bytes 2674948
  48.2 1.9 copy-start.11
  48.2 1.9 copy-start.12
  48.2 1.9 copy-start.23
  48.2 1.9 copy-start.24
  48.2 1.9 copy-start.25
  50.1 1.0 copy-start.9
  50.1 1.2 copy-start.17
  50.1 1.3 copy-start.18
  50.1 1.5 copy-start.19
  51.6 40.1 %copy-start.31 = (f32[16]{0:T(128)S(1)}, f32[16]{0:T(128)}, u32[]{:S(2)}) copy-start(f32[16]{0:T(128)} %param.7) | copy-start | bytes 196
  51.6 40.1 %copy-start.32 = (f32[16]{0:T(128)S(1)}, f32[16]{0:T(128)}, u32[]{:S(2)}) copy-start(f32[16]{0:T(128)} %param.8) | copy-start | bytes 196
  52.8 81.8 %copy-start.4 = (f32[16,4,16,128]{3,0,2,1:T(8,128)}, f32[16,4,16,128]{3,0,2,1:T(8,128)S(1)}, u32[]{:S(2)}) copy-start(f32[16,4,16,128]{3,0,2,1:T(8,128)S(1)} %get-tuple-element.47) | copy-start | bytes 1572868
  134.6 3.7 %copy-start.33 = (f32[16]{0:T(128)}, f32[16]{0:T(128)S(1)}, u32[]{:S(2)}) copy-start(f32[16]{0:T(128)S(1)} %get-tuple-element.16) | copy-start | bytes 196
  134.6 3.7 %copy-start.34 = (f32[16]{0:T(128)}, f32[16]{0:T(128)S(1)}, u32[]{:S(2)}) copy-start(f32[16]{0:T(128)S(1)} %get-tuple-element.17) | copy-start | bytes 196
  136.0 2.3 copy-start.1
  137.5 2.5 %copy-start.8 = (f32[16,5,16,128]{3,0,2,1:T(8,128)S(1)}, f32[16,5,16,128]{3,0,2,1:T(8,128)}, u32[]{:S(2)}) copy-start(f32[16,5,16,128]{3,0,2,1:T(8,128)} %copy-done.7) | copy-start | bytes 1966084
  145.0 2.5 copy-start.3
  152.6 2.5 %copy-start.6 = (f32[16,5,16,128]{3,0,2,1:T(8,128)S(1)}, f32[16,5,16,128]{3,0,2,1:T(8,128)}, u32[]{:S(2)}) copy-start(f32[16,5,16,128]{3,0,2,1:T(8,128)} %copy-done.5) | copy-start | bytes 1966084
  157.0 47.2 %copy-start.27 = (f32[16,16,3,3,3]{1,0,4,3,2:T(8,128)S(1)}, f32[16,16,3,3,3]{1,0,4,3,2:T(8,128)}, u32[]{:S(2)}) copy-start(f32[16,16,3,3,3]{1,0,4,3,2:T(8,128)} %param.6) | copy-start | bytes 82948
  157.8 44.3 %copy-start.30 = (f32[16,1,16,128]{3,0,2,1:T(8,128)S(1)}, f32[16,1,16,128]{3,0,2,1:T(8,128)}, u32[]{:S(2)}) copy-start(f32[16,1,16,128]{3,0,2,1:T(8,128)} %get-tuple-element.35) | copy-start | bytes 393220
  157.8 45.9 %copy-start.29 = (f32[16,1,16,128]{3,0,2,1:T(8,128)S(1)}, f32[16,1,16,128]{3,0,2,1:T(8,128)}, u32[]{:S(2)}) copy-start(f32[16,1,16,128]{3,0,2,1:T(8,128)} %get-tuple-element.36) | copy-start | bytes 393220
  159.5 0.7 copy-start.28
  202.1 5.9 %collective-permute-start.6 = (f32[16,1,16,128]{3,0,2,1:T(8,128)S(1)}, f32[16,1,16,128]{3,0,2,1:T(8,128)S(1)}, u32[]{:S(2)}, u32[]{:S(2)}) collective-permute-start(f32[16,1,16,128]{3,0,2,1:T(8,128)S(1)} %copy-done.30), channel_id=1, source_target_pairs={{0,16},{16,0},{1,17},{17,1},{2,18},{18,2},{3,19},{19,3},{4,20},{20... | collective-permute-start | bytes 393224 | tf_op jit(solution)/shard_map/ppermute | solution.py:13
  203.7 5.7 %collective-permute-start.7 = (f32[16,1,16,128]{3,0,2,1:T(8,128)S(1)}, f32[16,1,16,128]{3,0,2,1:T(8,128)S(1)}, u32[]{:S(2)}, u32[]{:S(2)}) collective-permute-start(f32[16,1,16,128]{3,0,2,1:T(8,128)S(1)} %copy-done.29), channel_id=1, source_target_pairs={{16,0},{0,16},{17,1},{1,17},{18,2},{2,18},{19,3},{3,19},{20,4},{4,... | collective-permute-start | bytes 393224 | tf_op jit(solution)/shard_map/ppermute | solution.py:16
  209.4 4.2 %collective-permute-start.9 = (f32[16,6,1,128]{3,0,2,1:T(8,128)S(1)}, f32[16,6,1,128]{3,0,2,1:T(8,128)S(1)}, u32[]{:S(2)}, u32[]{:S(2)}) collective-permute-start(f32[16,6,1,128]{3,0,2,1:T(8,128)S(1)} %get-tuple-element.32), channel_id=1, source_target_pairs={{4,0},{8,4},{12,8},{0,12},{5,1},{9,5},{13,9},{1,13},{6,2},{10,6},{... | collective-permute-start | bytes 147464 | tf_op jit(solution)/shard_map/ppermute | solution.py:16
  211.7 5.9 %collective-permute-start.8 = (f32[16,6,1,128]{3,0,2,1:T(8,128)S(1)}, f32[16,6,1,128]{3,0,2,1:T(8,128)S(1)}, u32[]{:S(2)}, u32[]{:S(2)}) collective-permute-start(f32[16,6,1,128]{3,0,2,1:T(8,128)S(1)} %get-tuple-element.31), channel_id=1, source_target_pairs={{0,4},{4,8},{8,12},{12,0},{1,5},{5,9},{9,13},{13,1},{2,6},{6,10},{... | collective-permute-start | bytes 147464 | tf_op jit(solution)/shard_map/ppermute | solution.py:13
  220.7 9.7 %collective-permute-start.10 = (f32[16,6,18,1]{2,0,3,1:T(8,128)S(1)}, f32[16,6,18,1]{2,0,3,1:T(8,128)S(1)}, u32[]{:S(2)}, u32[]{:S(2)}) collective-permute-start(f32[16,6,18,1]{2,0,3,1:T(8,128)S(1)} %copy.56), channel_id=1, source_target_pairs={{1,0},{2,1},{3,2},{0,3},{5,4},{6,5},{7,6},{4,7},{9,8},{10,9},{11,1... | collective-permute-start | bytes 20744 | tf_op jit(solution)/shard_map/ppermute | solution.py:16
  221.4 10.6 %collective-permute-start.11 = (f32[16,6,18,1]{2,0,3,1:T(8,128)S(1)}, f32[16,6,18,1]{2,0,3,1:T(8,128)S(1)}, u32[]{:S(2)}, u32[]{:S(2)}) collective-permute-start(f32[16,6,18,1]{2,0,3,1:T(8,128)S(1)} %copy.60), channel_id=1, source_target_pairs={{0,1},{1,2},{2,3},{3,0},{4,5},{5,6},{6,7},{7,4},{8,9},{9,10},{10,1... | collective-permute-start | bytes 20744 | tf_op jit(solution)/shard_map/ppermute | solution.py:13
  244.1 2.3 copy-start.10
  244.1 2.3 copy-start.13
  244.1 2.3 copy-start.20
  244.3 2.1 copy-start.21
  244.3 2.1 copy-start.22
  246.4 1.1 copy-start.14
  246.4 1.2 copy-start.15
  246.4 1.3 copy-start.16
where the time goes:
time: 255 us; the launch traced here: 250 us
  blocking collectives  121 us (47%)
  matrix products  78.7 us (31%)
  local copies, waits for them, and re-layouts  15.7 us (6%)
  starting transfers between devices  13.8 us (5%)
  waiting for transfers between devices  10.9 us (4%)
  other arithmetic  7.77 us (3%)
    dot_general x54, matrix products, mix(): jnp.einsum('oi,ixyz->oxyz', kernel, slab, precision=lax.Precision.HIGHEST)  56 us
    psum x1, blocking collectives, shards(): lax.psum(jnp.stack(pieces, axis=2).reshape(chans, chans, 3, 3, 3), ('gx',...  41.9 us
    psum x1, blocking collectives, shards(): lax.psum((jnp.sum(act_grad * normed, axis=(1, 2, 3)), jnp.sum(act_grad, a...  40.5 us
    psum x1, blocking collectives, shards(): lax.psum((jnp.sum(conv, axis=(1, 2, 3)), jnp.sum(conv * conv, axis=(1, 2,...  38.9 us
    dot_general x27, matrix products, contract(): jnp.einsum('oxyz,ixyz->oi', left, slab, precision=lax.Precision.HIGHEST)  22.7 us
    ppermute x6, waiting for transfers between devices, with_halo(): lax.ppermute(lax.slice_in_dim(block, block.shape[dim] - width, None, axis...  7.88 us
    ppermute x6, starting transfers between devices, with_halo(): lax.ppermute(lax.slice_in_dim(block, block.shape[dim] - width, None, axis...  7.03 us
    ppermute x6, starting transfers between devices, with_halo(): lax.ppermute(lax.slice_in_dim(block, 0, width, axis=dim), axis, backward)  6.81 us
  transfers between devices with their start and end apart: 12, of which 5 were waited for; matrix products, arithmetic and copies ran while one was open for 14% of the time, Pallas kernels for 0%

commit v1 on v0

--- a/solution.py
+++ b/solution.py
@@ -2,6 +2,11 @@
 import jax.numpy as jnp
 from jax import lax
 from jax.sharding import PartitionSpec as P
+
+
+def axis_by_axis(array, inner_axis, outer_axis):
+    partial = lax.psum(array, inner_axis)
+    return lax.psum(partial, outer_axis)
 
 
 def with_halo(block, sides, width):
@@ -50,8 +55,8 @@
                 conv = conv + mix(
                     weight[:, :, first, second, third], window(padded, first, second, third)
                 )
-    first_sum, square_sum = lax.psum(
-        (jnp.sum(conv, axis=(1, 2, 3)), jnp.sum(conv * conv, axis=(1, 2, 3))), ("gx", "gy", "gz")
+    first_sum, square_sum = axis_by_axis(
+        (jnp.sum(conv, axis=(1, 2, 3)), jnp.sum(conv * conv, axis=(1, 2, 3))), ("gy", "gz"), "gx"
     )
     mean = first_sum / count
     var = square_sum / count - mean * mean

time: 255 us -> 250 us (0.980)
  blocking collectives: 121 us -> 117 us
    psum x1, blocking collectives: 40.5 us -> 36.9 us  [shards(): lax.psum((jnp.sum(act_grad * normed, axis=(1, 2, 3)), jnp.sum(act_grad, a...]
    psum x1 -> x2, blocking collectives: 38.9 us -> 35.8 us  [the longest x1 30.9 us: axis_by_axis(): partial = lax.psum(array, inner_axis)]
    psum x1, blocking collectives: 41.9 us -> 44.8 us  [shards(): lax.psum(jnp.stack(pieces, axis=2).reshape(chans, chans, 3, 3, 3), ('gx',...]
  transfers between devices with their start and end apart: 12 -> 12, of which waited for: 5 -> 6; matrix products, arithmetic and copies ran while one was open for 14% -> 14% of each run, Pallas kernels for 0% -> 0%
where the time goes in v1:
time: 250 us; the launch traced here: 246 us
  blocking collectives  117 us (47%)
  matrix products  78.7 us (31%)
  local copies, waits for them, and re-layouts  15.7 us (6%)
  starting transfers between devices  13.7 us (5%)
  waiting for transfers between devices  10.3 us (4%)
  other arithmetic  7.77 us (3%)
    dot_general x54, matrix products, mix(): jnp.einsum('oi,ixyz->oxyz', kernel, slab, precision=lax.Precision.HIGHEST)  56 us
    psum x1, blocking collectives, shards(): lax.psum(jnp.stack(pieces, axis=2).reshape(chans, chans, 3, 3, 3), ('gx',...  44.8 us
    psum x1, blocking collectives, shards(): lax.psum((jnp.sum(act_grad * normed, axis=(1, 2, 3)), jnp.sum(act_grad, a...  36.9 us
    psum x1, blocking collectives, axis_by_axis(): partial = lax.psum(array, inner_axis)  30.9 us
    dot_general x27, matrix products, contract(): jnp.einsum('oxyz,ixyz->oi', left, slab, precision=lax.Precision.HIGHEST)  22.7 us
    ppermute x6, starting transfers between devices, with_halo(): lax.ppermute(lax.slice_in_dim(block, block.shape[dim] - width, None, axis...  7.46 us
    ppermute x6, waiting for transfers between devices, with_halo(): lax.ppermute(lax.slice_in_dim(block, block.shape[dim] - width, None, axis...  6.79 us
    ppermute x6, starting transfers between devices, with_halo(): lax.ppermute(lax.slice_in_dim(block, 0, width, axis=dim), axis, backward)  6.23 us
  transfers between devices with their start and end apart: 12, of which 6 were waited for; matrix products, arithmetic and copies ran while one was open for 14% of the time, Pallas kernels for 0%

profile of v1, /device:TPU:0, one launch (start us, length us, event | category | flops | bytes accessed | tf_op | source)
XLA Modules:
  0.0 245.5 jit_solution(5017022611118090781)
XLA Ops:
  0.6 1.1 fusion.319
  1.7 3.0 %collective-permute-start = (f32[16,1,16,128]{3,0,2,1:T(8,128)S(1)}, f32[16,1,16,128]{3,0,2,1:T(8,128)S(1)}, u32[]{:S(2)}, u32[]{:S(2)}) collective-permute-start(f32[16,1,16,128]{3,0,2,1:T(8,128)S(1)} %copy.207), channel_id=1, source_target_pairs={{0,16},{16,0},{1,17},{17,1},{2,18},{18,2},{3,19},{19,3},{4,20},{20... | collective-permute-start | bytes 393224 | tf_op jit(solution)/shard_map/ppermute | solution.py:18
  4.9 2.7 %fusion.206 = f32[16,4,16,128]{3,0,2,1:T(8,128)} fusion(f32[16,16,3,3,3]{1,0,4,3,2:T(8,128)} %param.6, f32[16,4,16,128]{3,2,1,0:T(8,128)} %param.5), kind=kOutput, calls=%fused_computation.290 | convolution fusion | flops 25165824 | bytes 1056768 | tf_op jit(solution)/shard_map/oi,ixyz->oxyz/dot_general | solution.py:27
  7.6 1.5 collective-permute-done
  9.5 1.6 collective-permute-done.1
  11.1 1.9 collective-permute-start.2
  13.0 2.1 collective-permute-start.3
  15.1 2.1 fusion.225
  17.2 2.1 convolution_bitcast_fusion.4
  21.0 1.9 collective-permute-start.5
  23.0 2.1 fusion.85
  25.0 2.0 fusion.86
  27.1 2.1 fusion.87
  29.1 2.1 convolution_bitcast_fusion.3
  31.2 2.1 convolution_bitcast_fusion.5
  33.3 2.1 convolution_bitcast_fusion.6
  36.1 1.6 copy.51
  37.7 1.8 maximum_maximum_fusion
  47.1 1.1 convolution_bitcast_fusion.18
  51.6 1.2 fusion.312
  52.8 30.9 %all-reduce.1 = (f32[16]{0:T(128)S(1)}, f32[16]{0:T(128)S(1)}) all-reduce(f32[16]{0:T(128)S(1)} %get-tuple-element.15, f32[16]{0:T(128)S(1)} %get-tuple-element.14), channel_id=1, replica_groups=mesh['gx'=2,'gy'=4,'gz'=4] {'gy','gz'}, use_global_device_ids=true, to_apply=%region_1.0 | all-reduce | flops 32 | bytes 256 | tf_op jit(solution)/shard_map/psum | solution.py:8
  83.7 4.9 %all-reduce.2 = (f32[16]{0:T(128)S(1)}, f32[16]{0:T(128)S(1)}) all-reduce(f32[16]{0:T(128)S(1)} %get-tuple-element.18, f32[16]{0:T(128)S(1)} %get-tuple-element.19), channel_id=1, replica_groups=mesh['gx'=2,'gy'=4,'gz'=4] {'gx'}, use_global_device_ids=true, to_apply=%region_2.0 | all-reduce | flops 32 | bytes 256 | tf_op jit(solution)/shard_map/psum | solution.py:9
  88.6 2.4 fusion.311
  91.0 36.9 %all-reduce = (f32[16]{0:T(128)S(1)}, f32[16]{0:T(128)S(1)}) all-reduce(f32[16]{0:T(128)S(1)} %get-tuple-element.13, f32[16]{0:T(128)S(1)} %get-tuple-element.12), channel_id=1, replica_groups=mesh['gx'=2,'gy'=4,'gz'=4] {'gx','gy','gz'}, use_global_device_ids=true, to_apply=%region_9.0 | all-reduce | flops 32 | bytes 256 | tf_op jit(solution)/shard_map/psum | solution.py:70
  127.9 1.4 subtract_multiply_fusion
  140.8 1.0 fusion.64
  148.4 1.0 fusion.55
  153.5 44.8 %psum.55 = f32[16,16,3,3,3]{1,0,4,3,2:T(8,128)} all-reduce(f32[16,16,3,3,3]{1,0,4,3,2:T(8,128)} %bitcast.644), channel_id=1, replica_groups=mesh['gx'=2,'gy'=4,'gz'=4] {'gx','gy','gz'}, use_global_device_ids=true, to_apply=%region_10.0 | all-reduce | flops 6912 | bytes 55296 | tf_op jit(solution)/shard_map/psum | solution.py:84
  198.3 1.5 collective-permute-start.6
  200.3 1.4 fusion.204
  201.7 2.4 collective-permute-done.6
  204.2 1.4 collective-permute-done.7
  205.6 1.6 collective-permute-start.9
  207.7 1.4 fusion.78
  210.2 2.8 %collective-permute-done.8 = f32[16,6,1,128]{3,0,2,1:T(8,128)S(1)} collective-permute-done((f32[16,6,1,128]{3,0,2,1:T(8,128)S(1)}, f32[16,6,1,128]{3,0,2,1:T(8,128)S(1)}, u32[]{:S(2)}, u32[]{:S(2)}) %collective-permute-start.8) | collective-permute-done | bytes 49184 | tf_op jit(solution)/shard_map/ppermute | solution.py:18
  213.1 1.2 fusion.315
  214.4 1.8 copy.56
  217.4 1.4 fusion.177
  218.8 1.4 fusion.175
  220.2 1.4 fusion.176
  221.7 1.4 fusion.174
  223.1 1.4 convolution_bitcast_fusion.2
  224.5 1.4 convolution_bitcast_fusion
  225.9 1.6 copy.57
  227.5 1.6 copy.61
  229.1 2.0 pad_maximum_fusion.3
  242.0 1.1 fusion.46
  243.4 1.0 fusion.48
  (159 shorter events, 51.1 us)
Async XLA Ops:
  0.6 8.5 %copy-start.2 = (f32[16,4,16,128]{3,2,1,0:T(8,128)S(1)}, f32[16,4,16,128]{3,2,1,0:T(8,128)}, u32[]{:S(2)}) copy-start(f32[16,4,16,128]{3,2,1,0:T(8,128)} %param.5) | copy-start | bytes 1572868
  1.7 7.4 %collective-permute-start = (f32[16,1,16,128]{3,0,2,1:T(8,128)S(1)}, f32[16,1,16,128]{3,0,2,1:T(8,128)S(1)}, u32[]{:S(2)}, u32[]{:S(2)}) collective-permute-start(f32[16,1,16,128]{3,0,2,1:T(8,128)S(1)} %copy.207), channel_id=1, source_target_pairs={{0,16},{16,0},{1,17},{17,1},{2,18},{18,2},{3,19},{19,3},{4,20},{20... | collective-permute-start | bytes 393224 | tf_op jit(solution)/shard_map/ppermute | solution.py:18
  4.8 6.3 %collective-permute-start.1 = (f32[16,1,16,128]{3,0,2,1:T(8,128)S(1)}, f32[16,1,16,128]{3,0,2,1:T(8,128)S(1)}, u32[]{:S(2)}, u32[]{:S(2)}) collective-permute-start(f32[16,1,16,128]{3,0,2,1:T(8,128)S(1)} %copy.208), channel_id=1, source_target_pairs={{16,0},{0,16},{17,1},{1,17},{18,2},{2,18},{19,3},{3,19},{20,4},{4,... | collective-permute-start | bytes 393224 | tf_op jit(solution)/shard_map/ppermute | solution.py:21
  9.5 9.8 %copy-start.7 = (f32[16,5,16,128]{3,0,2,1:T(8,128)}, f32[16,5,16,128]{3,0,2,1:T(8,128)S(1)}, u32[]{:S(2)}) copy-start(f32[16,5,16,128]{3,0,2,1:T(8,128)S(1)} %get-tuple-element.39) | copy-start | bytes 1966084
  11.1 8.1 %copy-start.5 = (f32[16,5,16,128]{3,0,2,1:T(8,128)}, f32[16,5,16,128]{3,0,2,1:T(8,128)S(1)}, u32[]{:S(2)}) copy-start(f32[16,5,16,128]{3,0,2,1:T(8,128)S(1)} %get-tuple-element.46) | copy-start | bytes 1966084
  11.1 8.1 %collective-permute-start.2 = (f32[16,6,1,128]{3,0,2,1:T(8,128)S(1)}, f32[16,6,1,128]{3,0,2,1:T(8,128)S(1)}, u32[]{:S(2)}, u32[]{:S(2)}) collective-permute-start(f32[16,6,1,128]{3,0,2,1:T(8,128)S(1)} %get-tuple-element.35), channel_id=1, source_target_pairs={{0,4},{4,8},{8,12},{12,0},{1,5},{5,9},{9,13},{13,1},{2,6},{6,10},{... | collective-permute-start | bytes 147464 | tf_op jit(solution)/shard_map/ppermute | solution.py:18
  13.0 6.2 %collective-permute-start.3 = (f32[16,6,1,128]{3,0,2,1:T(8,128)S(1)}, f32[16,6,1,128]{3,0,2,1:T(8,128)S(1)}, u32[]{:S(2)}, u32[]{:S(2)}) collective-permute-start(f32[16,6,1,128]{3,0,2,1:T(8,128)S(1)} %get-tuple-element.36), channel_id=1, source_target_pairs={{4,0},{8,4},{12,8},{0,12},{5,1},{9,5},{13,9},{1,13},{6,2},{10,6},{... | collective-permute-start | bytes 147464 | tf_op jit(solution)/shard_map/ppermute | solution.py:21
  20.3 15.0 %collective-permute-start.4 = (f32[16,6,18,1]{2,0,3,1:T(8,128)S(1)}, f32[16,6,18,1]{2,0,3,1:T(8,128)S(1)}, u32[]{:S(2)}, u32[]{:S(2)}) collective-permute-start(f32[16,6,18,1]{2,0,3,1:T(8,128)S(1)} %copy.48), channel_id=1, source_target_pairs={{0,1},{1,2},{2,3},{3,0},{4,5},{5,6},{6,7},{7,4},{8,9},{9,10},{10,1... | collective-permute-start | bytes 20744 | tf_op jit(solution)/shard_map/ppermute | solution.py:18
  21.0 15.0 %collective-permute-start.5 = (f32[16,6,18,1]{2,0,3,1:T(8,128)S(1)}, f32[16,6,18,1]{2,0,3,1:T(8,128)S(1)}, u32[]{:S(2)}, u32[]{:S(2)}) collective-permute-start(f32[16,6,18,1]{2,0,3,1:T(8,128)S(1)} %copy.50), channel_id=1, source_target_pairs={{1,0},{2,1},{3,2},{0,3},{5,4},{6,5},{7,6},{4,7},{9,8},{10,9},{11,1... | collective-permute-start | bytes 20744 | tf_op jit(solution)/shard_map/ppermute | solution.py:21
  37.7 1.8 copy-start.26
  39.5 11.6 %copy-start = (f32[16,6,18,129]{3,0,2,1:T(8,128)}, f32[16,6,18,129]{3,0,2,1:T(8,128)S(1)}, u32[]{:S(2)}) copy-start(f32[16,6,18,129]{3,0,2,1:T(8,128)S(1)} %get-tuple-element.30) | copy-start | bytes 2674948
  48.2 1.9 copy-start.11
  48.2 1.9 copy-start.12
  48.2 1.9 copy-start.23
  48.2 1.9 copy-start.24
  48.2 1.9 copy-start.25
  50.1 1.0 copy-start.9
  50.1 1.2 copy-start.17
  50.1 1.3 copy-start.18
  50.1 1.5 copy-start.19
  51.6 37.0 %copy-start.31 = (f32[16]{0:T(128)S(1)}, f32[16]{0:T(128)}, u32[]{:S(2)}) copy-start(f32[16]{0:T(128)} %param.7) | copy-start | bytes 196
  51.6 37.0 %copy-start.32 = (f32[16]{0:T(128)S(1)}, f32[16]{0:T(128)}, u32[]{:S(2)}) copy-start(f32[16]{0:T(128)} %param.8) | copy-start | bytes 196
  52.8 75.1 %copy-start.4 = (f32[16,4,16,128]{3,0,2,1:T(8,128)}, f32[16,4,16,128]{3,0,2,1:T(8,128)S(1)}, u32[]{:S(2)}) copy-start(f32[16,4,16,128]{3,0,2,1:T(8,128)S(1)} %get-tuple-element.49) | copy-start | bytes 1572868
  127.9 3.7 %copy-start.33 = (f32[16]{0:T(128)}, f32[16]{0:T(128)S(1)}, u32[]{:S(2)}) copy-start(f32[16]{0:T(128)S(1)} %get-tuple-element.16) | copy-start | bytes 196
  127.9 3.7 %copy-start.34 = (f32[16]{0:T(128)}, f32[16]{0:T(128)S(1)}, u32[]{:S(2)}) copy-start(f32[16]{0:T(128)S(1)} %get-tuple-element.17) | copy-start | bytes 196
  129.3 2.3 copy-start.1
  130.8 2.5 %copy-start.8 = (f32[16,5,16,128]{3,0,2,1:T(8,128)S(1)}, f32[16,5,16,128]{3,0,2,1:T(8,128)}, u32[]{:S(2)}) copy-start(f32[16,5,16,128]{3,0,2,1:T(8,128)} %copy-done.7) | copy-start | bytes 1966084
  138.3 2.5 %copy-start.3 = (f32[16,4,16,128]{3,2,1,0:T(8,128)S(1)}, f32[16,4,16,128]{3,2,1,0:T(8,128)}, u32[]{:S(2)}) copy-start(f32[16,4,16,128]{3,2,1,0:T(8,128)} %param.5) | copy-start | bytes 1572868
  145.9 2.5 %copy-start.6 = (f32[16,5,16,128]{3,0,2,1:T(8,128)S(1)}, f32[16,5,16,128]{3,0,2,1:T(8,128)}, u32[]{:S(2)}) copy-start(f32[16,5,16,128]{3,0,2,1:T(8,128)} %copy-done.5) | copy-start | bytes 1966084
  150.3 50.0 %copy-start.27 = (f32[16,16,3,3,3]{1,0,4,3,2:T(8,128)S(1)}, f32[16,16,3,3,3]{1,0,4,3,2:T(8,128)}, u32[]{:S(2)}) copy-start(f32[16,16,3,3,3]{1,0,4,3,2:T(8,128)} %param.6) | copy-start | bytes 82948
  151.1 47.2 %copy-start.30 = (f32[16,1,16,128]{3,0,2,1:T(8,128)S(1)}, f32[16,1,16,128]{3,0,2,1:T(8,128)}, u32[]{:S(2)}) copy-start(f32[16,1,16,128]{3,0,2,1:T(8,128)} %get-tuple-element.37) | copy-start | bytes 393220
  151.1 48.7 %copy-start.29 = (f32[16,1,16,128]{3,0,2,1:T(8,128)S(1)}, f32[16,1,16,128]{3,0,2,1:T(8,128)}, u32[]{:S(2)}) copy-start(f32[16,1,16,128]{3,0,2,1:T(8,128)} %get-tuple-element.38) | copy-start | bytes 393220
  152.8 0.7 copy-start.28
  198.3 5.9 %collective-permute-start.6 = (f32[16,1,16,128]{3,0,2,1:T(8,128)S(1)}, f32[16,1,16,128]{3,0,2,1:T(8,128)S(1)}, u32[]{:S(2)}, u32[]{:S(2)}) collective-permute-start(f32[16,1,16,128]{3,0,2,1:T(8,128)S(1)} %copy-done.30), channel_id=1, source_target_pairs={{0,16},{16,0},{1,17},{17,1},{2,18},{18,2},{3,19},{19,3},{4,20},{20... | collective-permute-start | bytes 393224 | tf_op jit(solution)/shard_map/ppermute | solution.py:18
  199.8 5.7 %collective-permute-start.7 = (f32[16,1,16,128]{3,0,2,1:T(8,128)S(1)}, f32[16,1,16,128]{3,0,2,1:T(8,128)S(1)}, u32[]{:S(2)}, u32[]{:S(2)}) collective-permute-start(f32[16,1,16,128]{3,0,2,1:T(8,128)S(1)} %copy-done.29), channel_id=1, source_target_pairs={{16,0},{0,16},{17,1},{1,17},{18,2},{2,18},{19,3},{3,19},{20,4},{4,... | collective-permute-start | bytes 393224 | tf_op jit(solution)/shard_map/ppermute | solution.py:21
  205.6 4.7 %collective-permute-start.9 = (f32[16,6,1,128]{3,0,2,1:T(8,128)S(1)}, f32[16,6,1,128]{3,0,2,1:T(8,128)S(1)}, u32[]{:S(2)}, u32[]{:S(2)}) collective-permute-start(f32[16,6,1,128]{3,0,2,1:T(8,128)S(1)} %get-tuple-element.34), channel_id=1, source_target_pairs={{4,0},{8,4},{12,8},{0,12},{5,1},{9,5},{13,9},{1,13},{6,2},{10,6},{... | collective-permute-start | bytes 147464 | tf_op jit(solution)/shard_map/ppermute | solution.py:21
  207.2 5.9 %collective-permute-start.8 = (f32[16,6,1,128]{3,0,2,1:T(8,128)S(1)}, f32[16,6,1,128]{3,0,2,1:T(8,128)S(1)}, u32[]{:S(2)}, u32[]{:S(2)}) collective-permute-start(f32[16,6,1,128]{3,0,2,1:T(8,128)S(1)} %get-tuple-element.33), channel_id=1, source_target_pairs={{0,4},{4,8},{8,12},{12,0},{1,5},{5,9},{9,13},{13,1},{2,6},{6,10},{... | collective-permute-start | bytes 147464 | tf_op jit(solution)/shard_map/ppermute | solution.py:18
  216.2 9.7 %collective-permute-start.10 = (f32[16,6,18,1]{2,0,3,1:T(8,128)S(1)}, f32[16,6,18,1]{2,0,3,1:T(8,128)S(1)}, u32[]{:S(2)}, u32[]{:S(2)}) collective-permute-start(f32[16,6,18,1]{2,0,3,1:T(8,128)S(1)} %copy.56), channel_id=1, source_target_pairs={{1,0},{2,1},{3,2},{0,3},{5,4},{6,5},{7,6},{4,7},{9,8},{10,9},{11,1... | collective-permute-start | bytes 20744 | tf_op jit(solution)/shard_map/ppermute | solution.py:21
  216.9 10.6 %collective-permute-start.11 = (f32[16,6,18,1]{2,0,3,1:T(8,128)S(1)}, f32[16,6,18,1]{2,0,3,1:T(8,128)S(1)}, u32[]{:S(2)}, u32[]{:S(2)}) collective-permute-start(f32[16,6,18,1]{2,0,3,1:T(8,128)S(1)} %copy.60), channel_id=1, source_target_pairs={{0,1},{1,2},{2,3},{3,0},{4,5},{5,6},{6,7},{7,4},{8,9},{9,10},{10,1... | collective-permute-start | bytes 20744 | tf_op jit(solution)/shard_map/ppermute | solution.py:18
  239.7 2.3 copy-start.10
  239.7 2.3 copy-start.13
  239.7 2.3 copy-start.20
  239.9 2.1 copy-start.21
  239.9 2.1 copy-start.22
  242.0 1.1 copy-start.14
  242.0 1.2 copy-start.15
  242.0 1.3 copy-start.16
